TPU v7x, 512 devices: a whole 4x8x8 slice. The times are simulated.
512 devices in a mesh: lat: 16 (over y_lo, x, core), lon: 32 (over y_hi, z).
Axes of the slice: x: 4, y: 8 (y_hi: 4, y_lo: 2; y = y_hi * 2 + y_lo), z: 8, core: 2. Of those that a mesh axis runs over, the one named last changes fastest.
Arguments:
- state_block: float32 [64, 1440, 256], P('lat', 'lon'), may hold values from -5 to 5
- stored_fields: bfloat16 [64, 1440, 1024], P('lat', 'lon'), may hold values from -14 to 14
- slope_fields: bfloat16 [64, 1440, 192], P('lat', 'lon'), may hold values from 0.5 to 1.5
- kernels: bfloat16 [3, 9, 64, 64], replicated, may hold values from -0.25 to 0.25
- spectral_gains: float32 [64, 721], replicated, may hold values from 0.25 to 4
Outputs:
- next_block: float32 [64, 1440, 256], P('lat', 'lon')
- diag_coef: float32 [4, 4], replicated
- stored_coef: float32 [16, 4], replicated
- norm_factor: float32 [4, 4], replicated
All inputs are finite; a program needn't handle non-finite values.
Results may differ from a plain program's by a relative error of at most 0.0062.
Values may be sent and summed in bfloat16 or wider, within the bound.
No kernel may reach another device: no remote copies, remote signals or barrier semaphores. Data moves between devices by JAX's collectives and lax.ppermute only.
A program may use at most 64 MiB of HBM per device.

v0:
```python
import jax
import jax.numpy as jnp
from jax import lax
from jax.sharding import PartitionSpec as P

highest = lax.Precision.HIGHEST
triple = lax.Precision.HIGH


def with_halo(cells, sides, width, closed):
    for axis, dim in sides:
        count = lax.axis_size(axis)
        ends = count if closed else count - 1
        head = lax.slice_in_dim(cells, 0, width, axis=dim)
        tail = lax.slice_in_dim(cells, cells.shape[dim] - width, cells.shape[dim], axis=dim)
        cells = jnp.concatenate(
            [
                lax.ppermute(tail, axis, [(i, (i + 1) % count) for i in range(ends)]),
                cells,
                lax.ppermute(head, axis, [((i + 1) % count, i) for i in range(ends)]),
            ],
            axis=dim,
        )
    return cells


def upper_factor(gram_matrix):
    count = gram_matrix.shape[0]
    nothing = gram_matrix[0, 0] * 0.0
    entries = [[nothing for col in range(count)] for row in range(count)]
    for row in range(count):
        total = gram_matrix[row, row]
        for inner in range(row):
            total = total - entries[inner][row] * entries[inner][row]
        entries[row][row] = jnp.sqrt(total)
        for col in range(row + 1, count):
            value = gram_matrix[row, col]
            for inner in range(row):
                value = value - entries[inner][row] * entries[inner][col]
            entries[row][col] = value / entries[row][row]
    inverse = [[nothing for col in range(count)] for row in range(count)]
    for col in range(count):
        inverse[col][col] = 1.0 / entries[col][col]
        for row in range(col - 1, -1, -1):
            value = nothing
            for inner in range(row + 1, col + 1):
                value = value + entries[row][inner] * inverse[inner][col]
            inverse[row][col] = -value / entries[row][row]
    factor = jnp.stack([jnp.stack(line) for line in entries])
    inverted = jnp.stack([jnp.stack(line) for line in inverse])
    return (factor, inverted)


def widen_layer(field):
    wrapped = with_halo(field, (("lon", 1),), 1, True)
    return with_halo(wrapped, (("lat", 0),), 1, False)


def stencil(extended, matrix, out_rows, out_cols, adjoint):
    channels = matrix.shape[1]
    split = extended.reshape(extended.shape[0], extended.shape[1], -1, channels)
    pieces = []
    for row_step in range(3):
        for col_step in range(3):
            if adjoint:
                pieces.append(
                    split[
                        2 - row_step : 2 - row_step + out_rows,
                        2 - col_step : 2 - col_step + out_cols,
                    ]
                )
            else:
                pieces.append(split[row_step : row_step + out_rows, col_step : col_step + out_cols])
    stacked = jnp.concatenate(pieces, axis=3)
    return jnp.einsum("abvk,kd->abvd", stacked, matrix, preferred_element_type=jnp.float32)


def scaled(slope, values):
    product = slope.astype(jnp.float32)[:, :, None, :] * values
    return product.astype(jnp.bfloat16).reshape(values.shape[0], values.shape[1], -1)


def as_split(field, channels):
    return field.reshape(field.shape[0], field.shape[1], -1, channels).astype(jnp.float32)


def spectral(hidden, spectral_gains, channels):
    band_rows = hidden.shape[0]
    columns = lax.all_to_all(hidden, "lon", split_axis=2, concat_axis=1, tiled=True)
    full_lon = columns.shape[1]
    own_columns = columns.shape[2]
    frequency_count = spectral_gains.shape[1]
    lat_total = band_rows * lax.axis_size("lat")
    row_index = lax.axis_index("lat") * band_rows + jnp.arange(band_rows, dtype=jnp.int32)
    latitude = (row_index.astype(jnp.float32) + 0.5) / lat_total
    area_weight = jnp.cos(jnp.pi * (latitude - 0.5))
    weighted = columns.astype(jnp.float32) * area_weight[:, None, None]
    row_major = jnp.transpose(weighted, (0, 2, 1)).reshape(band_rows * own_columns, full_lon)
    points = jnp.arange(full_lon, dtype=jnp.int32)
    wave_index = jnp.arange(frequency_count, dtype=jnp.int32)
    phase_index = points[:, None] * wave_index[None, :] % full_lon
    angles = phase_index.astype(jnp.float32) * (2.0 * jnp.pi / full_lon)
    cosine = jnp.cos(angles)
    sine_table = jnp.sin(angles)
    forward_table = jnp.concatenate([cosine, -sine_table], axis=1)
    backward_table = jnp.concatenate([cosine.T, -sine_table.T], axis=0)
    spectrum = jnp.dot(row_major, forward_table, precision=triple)
    lead_channel = lax.axis_index("lon") * own_columns % channels
    chosen = lax.dynamic_slice(spectral_gains, (lead_channel, 0), (own_columns, frequency_count))
    edge_wave = (wave_index == 0) | (wave_index == full_lon // 2)
    wave_weight = jnp.where(edge_wave, 1.0 / full_lon, 2.0 / full_lon).astype(jnp.float32)
    factor = chosen * wave_weight[None, :]
    factor = jnp.concatenate([factor, factor], axis=1)
    factor_rows = jnp.broadcast_to(factor[None], (band_rows, own_columns, 2 * frequency_count))
    factor_rows = factor_rows.reshape(band_rows * own_columns, 2 * frequency_count)
    restored = jnp.dot(spectrum * factor_rows, backward_table, precision=triple)
    restored = restored.reshape(band_rows, own_columns, full_lon) * area_weight[:, None, None]
    restored = jnp.transpose(restored, (0, 2, 1)).astype(jnp.bfloat16)
    return lax.all_to_all(restored, "lon", split_axis=1, concat_axis=2, tiled=True)


def per_device(state_block, stored_fields, slope_fields, kernels, spectral_gains):
    band_rows, tile_cols, block_width = state_block.shape
    layers = kernels.shape[0]
    channels = kernels.shape[2]
    vectors = block_width // channels
    forward_mats = [kernels[layer].reshape(9 * channels, channels) for layer in range(layers)]
    adjoint_mats = [
        jnp.transpose(kernels[layer], (0, 2, 1)).reshape(9 * channels, channels)
        for layer in range(layers)
    ]
    hidden = state_block.astype(jnp.bfloat16)
    for layer in range(layers):
        extended = widen_layer(hidden)
        summed = stencil(extended, forward_mats[layer], band_rows, tile_cols, False)
        hidden = scaled(slope_fields[:, :, layer * channels : (layer + 1) * channels], summed)
    filtered = spectral(hidden, spectral_gains, channels)
    top_slope = slope_fields[:, :, (layers - 1) * channels : layers * channels]
    adjoint = scaled(top_slope, as_split(filtered, channels))
    for layer in range(layers - 1, 0, -1):
        extended = widen_layer(adjoint)
        summed = stencil(extended, adjoint_mats[layer], band_rows, tile_cols, True)
        adjoint = scaled(slope_fields[:, :, (layer - 1) * channels : layer * channels], summed)
    extended = widen_layer(adjoint)
    image = stencil(extended, adjoint_mats[0], band_rows, tile_cols, True)
    cells = band_rows * tile_cols
    weighting = 1.0 / (
        band_rows * lax.axis_size("lat") * tile_cols * lax.axis_size("lon") * channels
    )
    current = state_block.reshape(cells, vectors, channels)
    stored = stored_fields.reshape(cells, -1, channels).astype(jnp.float32)
    image_cells = image.reshape(cells, vectors, channels)
    part_diag = jnp.einsum("xvc,xwc->vw", current, image_cells, precision=highest) * weighting
    part_stored = jnp.einsum("xsc,xwc->sw", stored, image_cells, precision=highest) * weighting
    diag_coef, stored_coef = lax.psum((part_diag, part_stored), ("lat", "lon"))
    residual = image_cells - jnp.einsum("xvc,vw->xwc", current, diag_coef, precision=highest)
    residual = residual - jnp.einsum("xsc,sw->xwc", stored, stored_coef, precision=highest)
    part_gram = jnp.einsum("xvc,xwc->vw", residual, residual, precision=highest) * weighting
    gram_matrix = lax.psum(part_gram, ("lat", "lon"))
    norm_factor, inverse = upper_factor(gram_matrix)
    next_fields = jnp.einsum("xvc,vw->xwc", residual, inverse, precision=highest)
    return (
        next_fields.reshape(band_rows, tile_cols, block_width),
        diag_coef,
        stored_coef,
        norm_factor,
    )


def solution(mesh):
    return jax.shard_map(
        per_device,
        mesh=mesh,
        in_specs=(P("lat", "lon", None), P("lat", "lon", None), P("lat", "lon", None), P(), P()),
        out_specs=(P("lat", "lon", None), P(), P(), P()),
        check_vma=False,
    )
```

profile of v0, /device:TPU:1, one launch (start us, length us, event | category | flops | bytes accessed | tf_op | source)
XLA Modules:
  0.0 468.9 jit_solution(3852663739283305581)
XLA Ops:
  1.6 5.0 %collective-permute-start = (bf16[4,1,256]{2,0,1:T(4,128)(2,1)S(1)}, bf16[4,1,256]{2,0,1:T(4,128)(2,1)S(1)}, u32[]{:S(2)}, u32[]{:S(2)}) collective-permute-start(bf16[4,1,256]{2,0,1:T(4,128)(2,1)S(1)} %get-tuple-element.115), channel_id=1, source_target_pairs={{0,1},{1,2},{2,3},{3,4},{4,5},{5,6},{6,7},{7,8},{8,9},{9,10},{10,1... | collective-permute-start | bytes 6152 | tf_op jit(solution)/shard_map/ppermute | solution.py:18
  6.6 12.4 %collective-permute-start.1 = (bf16[4,1,256]{2,0,1:T(4,128)(2,1)S(1)}, bf16[4,1,256]{2,0,1:T(4,128)(2,1)S(1)}, u32[]{:S(2)}, u32[]{:S(2)}) collective-permute-start(bf16[4,1,256]{2,0,1:T(4,128)(2,1)S(1)} %get-tuple-element.116), channel_id=1, source_target_pairs={{1,0},{2,1},{3,2},{4,3},{5,4},{6,5},{7,6},{8,7},{9,8},{10,9},{11,1... | collective-permute-start | bytes 6152 | tf_op jit(solution)/shard_map/ppermute | solution.py:20
  19.0 19.7 %sine_negate_fusion.1 = (f32[1440,721]{1,0:T(8,128)}, f32[1440,721]{1,0:T(8,128)}) fusion(), kind=kLoop, calls=%fused_computation.20 | loop fusion | flops 10382400 | bytes 8305920 | tf_op jit(solution)/shard_map/neg | solution.py:105
  39.8 4.0 collective-permute-start.2
  45.8 3.3 collective-permute-done.3
  54.8 19.8 %sine_negate_fusion = (f32[721,1440]{1,0:T(8,128)}, f32[721,1440]{1,0:T(8,128)}) fusion(), kind=kLoop, calls=%fused_computation.12 | loop fusion | flops 10382400 | bytes 8305920 | tf_op jit(solution)/shard_map/neg | solution.py:106
  74.5 7.6 %collective-permute-start.5 = (bf16[4,1,256]{2,0,1:T(4,128)(2,1)S(1)}, bf16[4,1,256]{2,0,1:T(4,128)(2,1)S(1)}, u32[]{:S(2)}, u32[]{:S(2)}) collective-permute-start(bf16[4,1,256]{2,0,1:T(4,128)(2,1)S(1)} %get-tuple-element.113), channel_id=1, source_target_pairs={{1,0},{2,1},{3,2},{4,3},{5,4},{6,5},{7,6},{8,7},{9,8},{10,9},{11,1... | collective-permute-start | bytes 6152 | tf_op jit(solution)/shard_map/ppermute | solution.py:20
  82.9 3.0 collective-permute-start.6
  87.9 3.4 collective-permute-done.7
  97.7 8.1 %collective-permute-start.9 = (bf16[4,1,256]{2,0,1:T(4,128)(2,1)S(1)}, bf16[4,1,256]{2,0,1:T(4,128)(2,1)S(1)}, u32[]{:S(2)}, u32[]{:S(2)}) collective-permute-start(bf16[4,1,256]{2,0,1:T(4,128)(2,1)S(1)} %get-tuple-element.108), channel_id=1, source_target_pairs={{1,0},{2,1},{3,2},{4,3},{5,4},{6,5},{7,6},{8,7},{9,8},{10,9},{11,1... | collective-permute-start | bytes 6152 | tf_op jit(solution)/shard_map/ppermute | solution.py:20
  106.6 2.7 collective-permute-start.10
  111.4 3.4 collective-permute-done.11
  119.4 8.3 %all-to-all-start = ((bf16[32,2,720]{2,1,0:T(2,128)(2,1)}), bf16[32,2,720]{2,1,0:T(2,128)(2,1)S(1)}, u32[]{:S(2)}, u32[]{:S(2)}) async-start(bf16[32,2,720]{2,1,0:T(2,128)(2,1)} %reshape.151), calls=%async_computation | async-start | bytes 196608 | tf_op jit(solution)/shard_map/all_to_all | solution.py:89
  127.8 11.2 %all-to-all-done = bf16[32,2,720]{2,1,0:T(2,128)(2,1)S(1)} async-done(((bf16[32,2,720]{2,1,0:T(2,128)(2,1)}), bf16[32,2,720]{2,1,0:T(2,128)(2,1)S(1)}, u32[]{:S(2)}, u32[]{:S(2)}) %all-to-all-start) | async-done | bytes 92192 | tf_op jit(solution)/shard_map/all_to_all | solution.py:89
  140.0 7.0 %fusion.20 = f32[32,1442]{1,0:T(8,128)S(1)} fusion(f32[1440,721]{1,0:T(8,128)} %get-tuple-element.127, f32[1440,721]{1,0:T(8,128)} %get-tuple-element.128, f32[4,1440,8]{1,2,0:T(8,128)S(1)} %reshape.130, f32[8,1442]{1,0:T(8,128)S(1)} %pad_maximum_fusion.8, f32[4]{0:T(128)S(1)} %multiply_cosine_fusion), kind=kOutput, calls=%fused_computation.26 | convolution fusion | flops 400852864 | bytes 8720976 | tf_op jit(solution)/shard_map/dot_general | solution.py:107
  147.0 5.2 %fusion.32 = bf16[4,1440,8]{1,2,0:T(8,128)(2,1)S(1)} fusion(f32[32,1442]{1,0:T(8,128)S(1)} %fusion.20, f32[721,1440]{1,0:T(8,128)S(1)} %bitcast.190, f32[721,1440]{1,0:T(8,128)} %get-tuple-element.130, f32[4]{0:T(128)S(1)} %multiply_cosine_fusion), kind=kOutput, calls=%fused_computation.30 | convolution fusion | flops 400852800 | bytes 8582672 | tf_op jit(solution)/shard_map/dot_general | solution.py:116
  153.9 1.9 reshape.153
  155.8 3.8 all-to-all-start.1
  160.0 11.6 %all-to-all-done.1 = bf16[32,2,720]{2,1,0:T(2,128)(2,1)S(1)} async-done(((bf16[32,2,720]{2,1,0:T(2,128)(2,1)}), bf16[32,2,720]{2,1,0:T(2,128)(2,1)S(1)}, u32[]{:S(2)}, u32[]{:S(2)}) %all-to-all-start.1) | async-done | bytes 92192 | tf_op jit(solution)/shard_map/all_to_all | solution.py:119
  176.1 2.7 collective-permute-start.12
  178.8 6.8 %collective-permute-start.13 = (bf16[4,1,256]{2,0,1:T(4,128)(2,1)S(1)}, bf16[4,1,256]{2,0,1:T(4,128)(2,1)S(1)}, u32[]{:S(2)}, u32[]{:S(2)}) collective-permute-start(bf16[4,1,256]{2,0,1:T(4,128)(2,1)S(1)} %get-tuple-element.107), channel_id=1, source_target_pairs={{1,0},{2,1},{3,2},{4,3},{5,4},{6,5},{7,6},{8,7},{9,8},{10,9},{11,1... | collective-permute-start | bytes 6152 | tf_op jit(solution)/shard_map/ppermute | solution.py:20
  186.5 5.5 %collective-permute-start.14 = (bf16[1,47,256]{2,0,1:T(2,128)(2,1)S(1)}, bf16[1,47,256]{2,0,1:T(2,128)(2,1)S(1)}, u32[]{:S(2)}, u32[]{:S(2)}) collective-permute-start(bf16[1,47,256]{2,0,1:T(2,128)(2,1)S(1)} %get-tuple-element.94), channel_id=1, source_target_pairs={{0,32},{32,64},{64,96},{96,128},{128,160},{160,192},{192,224},{224... | collective-permute-start | bytes 72200 | tf_op jit(solution)/shard_map/ppermute | solution.py:18
  192.0 2.1 collective-permute-start.15
  194.9 2.5 collective-permute-done.15
  203.0 8.1 %collective-permute-start.17 = (bf16[4,1,256]{2,0,1:T(4,128)(2,1)S(1)}, bf16[4,1,256]{2,0,1:T(4,128)(2,1)S(1)}, u32[]{:S(2)}, u32[]{:S(2)}) collective-permute-start(bf16[4,1,256]{2,0,1:T(4,128)(2,1)S(1)} %get-tuple-element.104), channel_id=1, source_target_pairs={{1,0},{2,1},{3,2},{4,3},{5,4},{6,5},{7,6},{8,7},{9,8},{10,9},{11,1... | collective-permute-start | bytes 6152 | tf_op jit(solution)/shard_map/ppermute | solution.py:20
  212.0 2.7 collective-permute-start.18
  217.4 2.7 collective-permute-done.19
  224.9 8.1 %collective-permute-start.21 = (bf16[4,1,256]{2,0,1:T(4,128)(2,1)S(1)}, bf16[4,1,256]{2,0,1:T(4,128)(2,1)S(1)}, u32[]{:S(2)}, u32[]{:S(2)}) collective-permute-start(bf16[4,1,256]{2,0,1:T(4,128)(2,1)S(1)} %get-tuple-element.102), channel_id=1, source_target_pairs={{1,0},{2,1},{3,2},{4,3},{5,4},{6,5},{7,6},{8,7},{9,8},{10,9},{11,1... | collective-permute-start | bytes 6152 | tf_op jit(solution)/shard_map/ppermute | solution.py:20
  233.8 2.7 collective-permute-start.22
  243.9 3.3 concatenate.83
  250.7 108.5 %all-reduce = (f32[16,4]{0,1:T(4,128)S(1)}, f32[4,4]{0,1:T(4,128)S(1)}) all-reduce(f32[16,4]{0,1:T(4,128)S(1)} %fusion.43, f32[4,4]{0,1:T(4,128)S(1)} %fusion.44), channel_id=1, replica_groups=mesh['lat'=16,'lon'=32] {'lat','lon'}, use_global_device_ids=true, to_apply=%region_1.2 | all-reduce | flops 80 | bytes 640 | tf_op jit(solution)/shard_map/psum | solution.py:155
  361.5 94.6 %psum.23 = f32[4,4]{1,0:T(4,128)S(1)} all-reduce(f32[4,4]{1,0:T(4,128)S(1)} %fusion.41), channel_id=1, replica_groups=mesh['lat'=16,'lon'=32] {'lat','lon'}, use_global_device_ids=true, to_apply=%region_2.3 | all-reduce | flops 16 | bytes 128 | tf_op jit(solution)/shard_map/psum | solution.py:159
  (213 shorter events, 67.0 us)
Async XLA Ops:
  1.6 37.1 %copy-start.3 = (bf16[3,9,64,64]{3,2,1,0:T(8,128)(2,1)S(1)}, bf16[3,9,64,64]{3,2,1,0:T(8,128)(2,1)}, u32[]{:S(2)}) copy-start(bf16[3,9,64,64]{3,2,1,0:T(8,128)(2,1)} %param.8) | copy-start | bytes 663556
  1.6 38.0 %collective-permute-start = (bf16[4,1,256]{2,0,1:T(4,128)(2,1)S(1)}, bf16[4,1,256]{2,0,1:T(4,128)(2,1)S(1)}, u32[]{:S(2)}, u32[]{:S(2)}) collective-permute-start(bf16[4,1,256]{2,0,1:T(4,128)(2,1)S(1)} %get-tuple-element.115), channel_id=1, source_target_pairs={{0,1},{1,2},{2,3},{3,4},{4,5},{5,6},{6,7},{7,8},{8,9},{9,10},{10,1... | collective-permute-start | bytes 6152 | tf_op jit(solution)/shard_map/ppermute | solution.py:18
  6.6 39.1 %copy-start.4 = (bf16[4,45,192]{2,0,1:T(4,128)(2,1)S(1)}, bf16[4,45,192]{2,0,1:T(4,128)(2,1)}, u32[]{:S(2)}) copy-start(bf16[4,45,192]{2,0,1:T(4,128)(2,1)} %param.7) | copy-start | bytes 207364
  6.6 33.0 %collective-permute-start.1 = (bf16[4,1,256]{2,0,1:T(4,128)(2,1)S(1)}, bf16[4,1,256]{2,0,1:T(4,128)(2,1)S(1)}, u32[]{:S(2)}, u32[]{:S(2)}) collective-permute-start(bf16[4,1,256]{2,0,1:T(4,128)(2,1)S(1)} %get-tuple-element.116), channel_id=1, source_target_pairs={{1,0},{2,1},{3,2},{4,3},{5,4},{6,5},{7,6},{8,7},{9,8},{10,9},{11,1... | collective-permute-start | bytes 6152 | tf_op jit(solution)/shard_map/ppermute | solution.py:20
  39.8 6.0 %collective-permute-start.2 = (bf16[1,47,256]{2,0,1:T(2,128)(2,1)S(1)}, bf16[1,47,256]{2,0,1:T(2,128)(2,1)S(1)}, u32[]{:S(2)}, u32[]{:S(2)}) collective-permute-start(bf16[1,47,256]{2,0,1:T(2,128)(2,1)S(1)} %get-tuple-element.100), channel_id=1, source_target_pairs={{0,32},{32,64},{64,96},{96,128},{128,160},{160,192},{192,224},{224... | collective-permute-start | bytes 72200 | tf_op jit(solution)/shard_map/ppermute | solution.py:18
  43.8 5.4 %collective-permute-start.3 = (bf16[1,47,256]{2,0,1:T(2,128)(2,1)S(1)}, bf16[1,47,256]{2,0,1:T(2,128)(2,1)S(1)}, u32[]{:S(2)}, u32[]{:S(2)}) collective-permute-start(bf16[1,47,256]{2,0,1:T(2,128)(2,1)S(1)} %get-tuple-element.101), channel_id=1, source_target_pairs={{32,0},{64,32},{96,64},{128,96},{160,128},{192,160},{224,192},{256... | collective-permute-start | bytes 72200 | tf_op jit(solution)/shard_map/ppermute | solution.py:20
  52.8 29.3 %collective-permute-start.4 = (bf16[4,1,256]{2,0,1:T(4,128)(2,1)S(1)}, bf16[4,1,256]{2,0,1:T(4,128)(2,1)S(1)}, u32[]{:S(2)}, u32[]{:S(2)}) collective-permute-start(bf16[4,1,256]{2,0,1:T(4,128)(2,1)S(1)} %get-tuple-element.114), channel_id=1, source_target_pairs={{0,1},{1,2},{2,3},{3,4},{4,5},{5,6},{6,7},{7,8},{8,9},{9,10},{10,1... | collective-permute-start | bytes 6152 | tf_op jit(solution)/shard_map/ppermute | solution.py:18
  74.5 8.3 %collective-permute-start.5 = (bf16[4,1,256]{2,0,1:T(4,128)(2,1)S(1)}, bf16[4,1,256]{2,0,1:T(4,128)(2,1)S(1)}, u32[]{:S(2)}, u32[]{:S(2)}) collective-permute-start(bf16[4,1,256]{2,0,1:T(4,128)(2,1)S(1)} %get-tuple-element.113), channel_id=1, source_target_pairs={{1,0},{2,1},{3,2},{4,3},{5,4},{6,5},{7,6},{8,7},{9,8},{10,9},{11,1... | collective-permute-start | bytes 6152 | tf_op jit(solution)/shard_map/ppermute | solution.py:20
  82.9 5.0 %collective-permute-start.6 = (bf16[1,47,256]{2,0,1:T(2,128)(2,1)S(1)}, bf16[1,47,256]{2,0,1:T(2,128)(2,1)S(1)}, u32[]{:S(2)}, u32[]{:S(2)}) collective-permute-start(bf16[1,47,256]{2,0,1:T(2,128)(2,1)S(1)} %get-tuple-element.98), channel_id=1, source_target_pairs={{0,32},{32,64},{64,96},{96,128},{128,160},{160,192},{192,224},{224... | collective-permute-start | bytes 72200 | tf_op jit(solution)/shard_map/ppermute | solution.py:18
  85.9 5.4 %collective-permute-start.7 = (bf16[1,47,256]{2,0,1:T(2,128)(2,1)S(1)}, bf16[1,47,256]{2,0,1:T(2,128)(2,1)S(1)}, u32[]{:S(2)}, u32[]{:S(2)}) collective-permute-start(bf16[1,47,256]{2,0,1:T(2,128)(2,1)S(1)} %get-tuple-element.99), channel_id=1, source_target_pairs={{32,0},{64,32},{96,64},{128,96},{160,128},{192,160},{224,192},{256... | collective-permute-start | bytes 72200 | tf_op jit(solution)/shard_map/ppermute | solution.py:20
  95.0 10.8 %collective-permute-start.8 = (bf16[4,1,256]{2,0,1:T(4,128)(2,1)S(1)}, bf16[4,1,256]{2,0,1:T(4,128)(2,1)S(1)}, u32[]{:S(2)}, u32[]{:S(2)}) collective-permute-start(bf16[4,1,256]{2,0,1:T(4,128)(2,1)S(1)} %get-tuple-element.109), channel_id=1, source_target_pairs={{0,1},{1,2},{2,3},{3,4},{4,5},{5,6},{6,7},{7,8},{8,9},{9,10},{10,1... | collective-permute-start | bytes 6152 | tf_op jit(solution)/shard_map/ppermute | solution.py:18
  97.7 8.8 %collective-permute-start.9 = (bf16[4,1,256]{2,0,1:T(4,128)(2,1)S(1)}, bf16[4,1,256]{2,0,1:T(4,128)(2,1)S(1)}, u32[]{:S(2)}, u32[]{:S(2)}) collective-permute-start(bf16[4,1,256]{2,0,1:T(4,128)(2,1)S(1)} %get-tuple-element.108), channel_id=1, source_target_pairs={{1,0},{2,1},{3,2},{4,3},{5,4},{6,5},{7,6},{8,7},{9,8},{10,9},{11,1... | collective-permute-start | bytes 6152 | tf_op jit(solution)/shard_map/ppermute | solution.py:20
  106.6 4.8 %collective-permute-start.10 = (bf16[1,47,256]{2,0,1:T(2,128)(2,1)S(1)}, bf16[1,47,256]{2,0,1:T(2,128)(2,1)S(1)}, u32[]{:S(2)}, u32[]{:S(2)}) collective-permute-start(bf16[1,47,256]{2,0,1:T(2,128)(2,1)S(1)} %get-tuple-element.96), channel_id=1, source_target_pairs={{0,32},{32,64},{64,96},{96,128},{128,160},{160,192},{192,224},{224... | collective-permute-start | bytes 72200 | tf_op jit(solution)/shard_map/ppermute | solution.py:18
  109.4 5.4 %collective-permute-start.11 = (bf16[1,47,256]{2,0,1:T(2,128)(2,1)S(1)}, bf16[1,47,256]{2,0,1:T(2,128)(2,1)S(1)}, u32[]{:S(2)}, u32[]{:S(2)}) collective-permute-start(bf16[1,47,256]{2,0,1:T(2,128)(2,1)S(1)} %get-tuple-element.97), channel_id=1, source_target_pairs={{32,0},{64,32},{96,64},{128,96},{160,128},{192,160},{224,192},{256... | collective-permute-start | bytes 72200 | tf_op jit(solution)/shard_map/ppermute | solution.py:20
  119.4 19.7 %all-to-all-start = ((bf16[32,2,720]{2,1,0:T(2,128)(2,1)}), bf16[32,2,720]{2,1,0:T(2,128)(2,1)S(1)}, u32[]{:S(2)}, u32[]{:S(2)}) async-start(bf16[32,2,720]{2,1,0:T(2,128)(2,1)} %reshape.151), calls=%async_computation | async-start | bytes 196608 | tf_op jit(solution)/shard_map/all_to_all | solution.py:89
  139.6 7.3 %slice-start = ((s8[4472832]{0:T(1024)(128)(4,1)}), s8[278528]{0:T(1024)(128)(4,1)S(1)}, s32[]{:S(2)}) async-start(s8[4472832]{0:T(1024)(128)(4,1)} %bitcast.189), calls=%async_computation.2 | async-start | bytes 557056
  153.9 40.3 %copy-start.1 = (bf16[9,64,64]{1,2,0:T(8,128)(2,1)S(1)}, bf16[9,64,64]{1,2,0:T(8,128)(2,1)}, u32[]{:S(2)}) copy-start(bf16[9,64,64]{1,2,0:T(8,128)(2,1)} %get-tuple-element.32) | copy-start | bytes 221188
  155.8 15.8 %all-to-all-start.1 = ((bf16[32,2,720]{2,1,0:T(2,128)(2,1)}), bf16[32,2,720]{2,1,0:T(2,128)(2,1)S(1)}, u32[]{:S(2)}, u32[]{:S(2)}) async-start(bf16[32,2,720]{2,1,0:T(2,128)(2,1)} %reshape.153), calls=%async_computation.1 | async-start | bytes 196608 | tf_op jit(solution)/shard_map/all_to_all | solution.py:119
  176.1 9.5 %collective-permute-start.12 = (bf16[4,1,256]{2,0,1:T(4,128)(2,1)S(1)}, bf16[4,1,256]{2,0,1:T(4,128)(2,1)S(1)}, u32[]{:S(2)}, u32[]{:S(2)}) collective-permute-start(bf16[4,1,256]{2,0,1:T(4,128)(2,1)S(1)} %get-tuple-element.106), channel_id=1, source_target_pairs={{0,1},{1,2},{2,3},{3,4},{4,5},{5,6},{6,7},{7,8},{8,9},{9,10},{10,1... | collective-permute-start | bytes 6152 | tf_op jit(solution)/shard_map/ppermute | solution.py:18
  178.8 7.6 %collective-permute-start.13 = (bf16[4,1,256]{2,0,1:T(4,128)(2,1)S(1)}, bf16[4,1,256]{2,0,1:T(4,128)(2,1)S(1)}, u32[]{:S(2)}, u32[]{:S(2)}) collective-permute-start(bf16[4,1,256]{2,0,1:T(4,128)(2,1)S(1)} %get-tuple-element.107), channel_id=1, source_target_pairs={{1,0},{2,1},{3,2},{4,3},{5,4},{6,5},{7,6},{8,7},{9,8},{10,9},{11,1... | collective-permute-start | bytes 6152 | tf_op jit(solution)/shard_map/ppermute | solution.py:20
  186.5 8.4 %collective-permute-start.14 = (bf16[1,47,256]{2,0,1:T(2,128)(2,1)S(1)}, bf16[1,47,256]{2,0,1:T(2,128)(2,1)S(1)}, u32[]{:S(2)}, u32[]{:S(2)}) collective-permute-start(bf16[1,47,256]{2,0,1:T(2,128)(2,1)S(1)} %get-tuple-element.94), channel_id=1, source_target_pairs={{0,32},{32,64},{64,96},{96,128},{128,160},{160,192},{192,224},{224... | collective-permute-start | bytes 72200 | tf_op jit(solution)/shard_map/ppermute | solution.py:18
  192.0 5.4 %collective-permute-start.15 = (bf16[1,47,256]{2,0,1:T(2,128)(2,1)S(1)}, bf16[1,47,256]{2,0,1:T(2,128)(2,1)S(1)}, u32[]{:S(2)}, u32[]{:S(2)}) collective-permute-start(bf16[1,47,256]{2,0,1:T(2,128)(2,1)S(1)} %get-tuple-element.95), channel_id=1, source_target_pairs={{32,0},{64,32},{96,64},{128,96},{160,128},{192,160},{224,192},{256... | collective-permute-start | bytes 72200 | tf_op jit(solution)/shard_map/ppermute | solution.py:20
  201.1 10.1 %collective-permute-start.16 = (bf16[4,1,256]{2,0,1:T(4,128)(2,1)S(1)}, bf16[4,1,256]{2,0,1:T(4,128)(2,1)S(1)}, u32[]{:S(2)}, u32[]{:S(2)}) collective-permute-start(bf16[4,1,256]{2,0,1:T(4,128)(2,1)S(1)} %get-tuple-element.105), channel_id=1, source_target_pairs={{0,1},{1,2},{2,3},{3,4},{4,5},{5,6},{6,7},{7,8},{8,9},{9,10},{10,1... | collective-permute-start | bytes 6152 | tf_op jit(solution)/shard_map/ppermute | solution.py:18
  203.0 8.8 %collective-permute-start.17 = (bf16[4,1,256]{2,0,1:T(4,128)(2,1)S(1)}, bf16[4,1,256]{2,0,1:T(4,128)(2,1)S(1)}, u32[]{:S(2)}, u32[]{:S(2)}) collective-permute-start(bf16[4,1,256]{2,0,1:T(4,128)(2,1)S(1)} %get-tuple-element.104), channel_id=1, source_target_pairs={{1,0},{2,1},{3,2},{4,3},{5,4},{6,5},{7,6},{8,7},{9,8},{10,9},{11,1... | collective-permute-start | bytes 6152 | tf_op jit(solution)/shard_map/ppermute | solution.py:20
  212.0 5.5 %collective-permute-start.18 = (bf16[1,47,256]{2,0,1:T(2,128)(2,1)S(1)}, bf16[1,47,256]{2,0,1:T(2,128)(2,1)S(1)}, u32[]{:S(2)}, u32[]{:S(2)}) collective-permute-start(bf16[1,47,256]{2,0,1:T(2,128)(2,1)S(1)} %get-tuple-element.92), channel_id=1, source_target_pairs={{0,32},{32,64},{64,96},{96,128},{128,160},{160,192},{192,224},{224... | collective-permute-start | bytes 72200 | tf_op jit(solution)/shard_map/ppermute | solution.py:18
  214.7 5.4 %collective-permute-start.19 = (bf16[1,47,256]{2,0,1:T(2,128)(2,1)S(1)}, bf16[1,47,256]{2,0,1:T(2,128)(2,1)S(1)}, u32[]{:S(2)}, u32[]{:S(2)}) collective-permute-start(bf16[1,47,256]{2,0,1:T(2,128)(2,1)S(1)} %get-tuple-element.93), channel_id=1, source_target_pairs={{32,0},{64,32},{96,64},{128,96},{160,128},{192,160},{224,192},{256... | collective-permute-start | bytes 72200 | tf_op jit(solution)/shard_map/ppermute | solution.py:20
  220.9 17.5 %copy-start = (f32[4,45,256]{2,0,1:T(4,128)S(1)}, f32[4,45,256]{2,0,1:T(4,128)}, u32[]{:S(2)}) copy-start(f32[4,45,256]{2,0,1:T(4,128)} %param.5) | copy-start | bytes 552964
  222.9 10.1 %collective-permute-start.20 = (bf16[4,1,256]{2,0,1:T(4,128)(2,1)S(1)}, bf16[4,1,256]{2,0,1:T(4,128)(2,1)S(1)}, u32[]{:S(2)}, u32[]{:S(2)}) collective-permute-start(bf16[4,1,256]{2,0,1:T(4,128)(2,1)S(1)} %get-tuple-element.103), channel_id=1, source_target_pairs={{0,1},{1,2},{2,3},{3,4},{4,5},{5,6},{6,7},{7,8},{8,9},{9,10},{10,1... | collective-permute-start | bytes 6152 | tf_op jit(solution)/shard_map/ppermute | solution.py:18
  224.9 8.8 %collective-permute-start.21 = (bf16[4,1,256]{2,0,1:T(4,128)(2,1)S(1)}, bf16[4,1,256]{2,0,1:T(4,128)(2,1)S(1)}, u32[]{:S(2)}, u32[]{:S(2)}) collective-permute-start(bf16[4,1,256]{2,0,1:T(4,128)(2,1)S(1)} %get-tuple-element.102), channel_id=1, source_target_pairs={{1,0},{2,1},{3,2},{4,3},{5,4},{6,5},{7,6},{8,7},{9,8},{10,9},{11,1... | collective-permute-start | bytes 6152 | tf_op jit(solution)/shard_map/ppermute | solution.py:20
  233.8 8.6 %collective-permute-start.22 = (bf16[1,47,256]{2,0,1:T(2,128)(2,1)S(1)}, bf16[1,47,256]{2,0,1:T(2,128)(2,1)S(1)}, u32[]{:S(2)}, u32[]{:S(2)}) collective-permute-start(bf16[1,47,256]{2,0,1:T(2,128)(2,1)S(1)} %get-tuple-element.90), channel_id=1, source_target_pairs={{0,32},{32,64},{64,96},{96,128},{128,160},{160,192},{192,224},{224... | collective-permute-start | bytes 72200 | tf_op jit(solution)/shard_map/ppermute | solution.py:18
  236.5 5.9 %collective-permute-start.23 = (bf16[1,47,256]{2,0,1:T(2,128)(2,1)S(1)}, bf16[1,47,256]{2,0,1:T(2,128)(2,1)S(1)}, u32[]{:S(2)}, u32[]{:S(2)}) collective-permute-start(bf16[1,47,256]{2,0,1:T(2,128)(2,1)S(1)} %get-tuple-element.91), channel_id=1, source_target_pairs={{32,0},{64,32},{96,64},{128,96},{160,128},{192,160},{224,192},{256... | collective-permute-start | bytes 72200 | tf_op jit(solution)/shard_map/ppermute | solution.py:20
  359.2 109.5 %copy-start.5 = (f32[16,4]{0,1:T(4,128)}, f32[16,4]{0,1:T(4,128)S(1)}, u32[]{:S(2)}) copy-start(f32[16,4]{0,1:T(4,128)S(1)} %get-tuple-element.28) | copy-start | bytes 772
  (2 other events, 8.8 us)
where the time goes:
time: 478 us; the launch traced here: 469 us
  blocking collectives  203 us (42%)
  starting transfers between devices  111 us (23%)
  other arithmetic  43.9 us (9%)
  waiting for transfers between devices  41.5 us (9%)
  local copies, waits for them, and re-layouts  35.2 us (7%)
  matrix products  24.3 us (5%)
  between operations  9.91 us (2%)
    psum x1, blocking collectives, per_device(): diag_coef, stored_coef = lax.psum((part_diag, part_stored), ('lat', 'lon'))  108 us
    psum x1, blocking collectives, per_device(): gram_matrix = lax.psum(part_gram, ('lat', 'lon'))  94.6 us
    ppermute x12, starting transfers between devices, with_halo(): lax.ppermute(head, axis, [((i + 1) % count, i) for i in range(ends)])  62.9 us
    ppermute x12, starting transfers between devices, with_halo(): lax.ppermute(tail, axis, [(i, (i + 1) % count) for i in range(ends)])  36 us
    neg x1, other arithmetic, spectral(): backward_table = jnp.concatenate([cosine.T, -sine_table.T], axis=0)  19.8 us
    neg x1, other arithmetic, spectral(): forward_table = jnp.concatenate([cosine, -sine_table], axis=1)  19.7 us
    ppermute x12, waiting for transfers between devices, with_halo(): lax.ppermute(head, axis, [((i + 1) % count, i) for i in range(ends)])  18.6 us
    all_to_all x1, waiting for transfers between devices, spectral(): lax.all_to_all(restored, 'lon', split_axis=1, concat_axis=2, tiled=True)  11.6 us
  transfers between devices with their start and end apart: 26, of which 12 were waited for; matrix products, arithmetic and copies ran while one was open for 10% of the time, Pallas kernels for 0%

commit v1 on v0

--- a/solution.py
+++ b/solution.py
@@ -156,7 +156,7 @@
     residual = image_cells - jnp.einsum("xvc,vw->xwc", current, diag_coef, precision=highest)
     residual = residual - jnp.einsum("xsc,sw->xwc", stored, stored_coef, precision=highest)
     part_gram = jnp.einsum("xvc,xwc->vw", residual, residual, precision=highest) * weighting
-    gram_matrix = lax.psum(part_gram, ("lat", "lon"))
+    gram_matrix = jnp.sum(lax.all_gather(part_gram, ("lat", "lon")), axis=0)
     norm_factor, inverse = upper_factor(gram_matrix)
     next_fields = jnp.einsum("xvc,vw->xwc", residual, inverse, precision=highest)
     return (

time: 478 us -> 1860 us (3.89)
  the two profiles are of different devices: /device:TPU:1 before, /device:TPU:8 now
where the time goes in v1:
time: 1860 us; the launch traced here: 1850 us
  blocking collectives  1570 us (84%)
  starting transfers between devices  126 us (7%)
  other arithmetic  44.5 us (2%)
  waiting for transfers between devices  37.2 us (2%)
  local copies, waits for them, and re-layouts  35.2 us (2%)
  matrix products  24.3 us (1%)
    all_gather x1, blocking collectives, per_device(): gram_matrix = jnp.sum(lax.all_gather(part_gram, ('lat', 'lon')), axis=0)  1480 us
    psum x1, blocking collectives, per_device(): diag_coef, stored_coef = lax.psum((part_diag, part_stored), ('lat', 'lon'))  97.3 us
    ppermute x12, starting transfers between devices, with_halo(): lax.ppermute(head, axis, [((i + 1) % count, i) for i in range(ends)])  86.8 us
  transfers between devices with their start and end apart: 26, of which 12 were waited for; matrix products, arithmetic and copies ran while one was open for 3% of the time, Pallas kernels for 0%

profile of v1, /device:TPU:8, one launch (start us, length us, event | category | flops | bytes accessed | tf_op | source)
XLA Modules:
  0.0 1849.4 jit_solution(4466769761318264082)
XLA Ops:
  1.6 4.4 collective-permute-start
  6.0 11.5 collective-permute-start.1
  17.6 19.7 %sine_negate_fusion.1 = (f32[1440,721]{1,0:T(8,128)}, f32[1440,721]{1,0:T(8,128)}) fusion(), kind=kLoop, calls=%fused_computation.20 | loop fusion | flops 10382400 | bytes 8305920 | tf_op jit(solution)/shard_map/neg | solution.py:105
  38.4 1.9 collective-permute-start.2
  40.3 5.8 collective-permute-start.3
  51.4 1.9 collective-permute-start.4
  53.4 19.8 %sine_negate_fusion = (f32[721,1440]{1,0:T(8,128)}, f32[721,1440]{1,0:T(8,128)}) fusion(), kind=kLoop, calls=%fused_computation.12 | loop fusion | flops 10382400 | bytes 8305920 | tf_op jit(solution)/shard_map/neg | solution.py:106
  73.1 8.1 collective-permute-start.5
  82.6 1.9 collective-permute-start.6
  84.6 5.8 collective-permute-start.7
  95.7 1.9 collective-permute-start.8
  98.4 8.4 collective-permute-start.9
  110.1 5.8 collective-permute-start.11
  122.2 8.6 all-to-all-start
  130.9 12.4 all-to-all-done
  144.2 7.0 fusion.20
  151.2 5.2 fusion.32
  158.1 1.9 reshape.157
  160.0 3.8 all-to-all-start.1
  164.2 12.1 all-to-all-done.1
  180.9 2.8 collective-permute-start.12
  183.7 7.3 collective-permute-start.13
  192.4 1.9 collective-permute-start.14
  194.3 5.9 collective-permute-start.15
  207.4 8.4 collective-permute-start.17
  219.1 5.8 collective-permute-start.19
  231.3 8.4 collective-permute-start.21
  241.1 1.9 collective-permute-start.22
  243.1 5.8 collective-permute-start.23
  254.3 3.3 concatenate.83
  261.1 97.3 %all-reduce = (f32[16,4]{0,1:T(4,128)S(1)}, f32[4,4]{0,1:T(4,128)S(1)}) all-reduce(f32[16,4]{0,1:T(4,128)S(1)} %fusion.43, f32[4,4]{0,1:T(4,128)S(1)} %fusion.45), channel_id=1, replica_groups=mesh['lat'=16,'lon'=32] {'lat','lon'}, use_global_device_ids=true, to_apply=%region_1.2 | all-reduce | flops 80 | bytes 640 | tf_op jit(solution)/shard_map/psum | solution.py:155
  360.6 1475.4 %all-gather.1 = f32[512,4,4]{2,1,0:T(4,128)S(1)} all-gather(f32[1,4,4]{2,1,0:T(4,128)S(1)} %fusion.44), channel_id=2, replica_groups=mesh['lat'=16,'lon'=32] {'lat','lon'}, dimensions={0}, use_global_device_ids=true | all-gather | bytes 32832 | tf_op jit(solution)/shard_map/all_gather | solution.py:159
  (214 shorter events, 67.4 us)
Async XLA Ops:
  1.6 35.7 %copy-start.3 = (bf16[3,9,64,64]{3,2,1,0:T(8,128)(2,1)S(1)}, bf16[3,9,64,64]{3,2,1,0:T(8,128)(2,1)}, u32[]{:S(2)}) copy-start(bf16[3,9,64,64]{3,2,1,0:T(8,128)(2,1)} %param.8) | copy-start | bytes 663556
  1.6 36.6 %collective-permute-start = (bf16[4,1,256]{2,0,1:T(4,128)(2,1)S(1)}, bf16[4,1,256]{2,0,1:T(4,128)(2,1)S(1)}, u32[]{:S(2)}, u32[]{:S(2)}) collective-permute-start(bf16[4,1,256]{2,0,1:T(4,128)(2,1)S(1)} %get-tuple-element.115), channel_id=1, source_target_pairs={{0,1},{1,2},{2,3},{3,4},{4,5},{5,6},{6,7},{7,8},{8,9},{9,10},{10,1... | collective-permute-start | bytes 6152 | tf_op jit(solution)/shard_map/ppermute | solution.py:18
  6.0 40.0 %copy-start.4 = (bf16[4,45,192]{2,0,1:T(4,128)(2,1)S(1)}, bf16[4,45,192]{2,0,1:T(4,128)(2,1)}, u32[]{:S(2)}) copy-start(bf16[4,45,192]{2,0,1:T(4,128)(2,1)} %param.7) | copy-start | bytes 207364
  6.0 32.1 %collective-permute-start.1 = (bf16[4,1,256]{2,0,1:T(4,128)(2,1)S(1)}, bf16[4,1,256]{2,0,1:T(4,128)(2,1)S(1)}, u32[]{:S(2)}, u32[]{:S(2)}) collective-permute-start(bf16[4,1,256]{2,0,1:T(4,128)(2,1)S(1)} %get-tuple-element.116), channel_id=1, source_target_pairs={{1,0},{2,1},{3,2},{4,3},{5,4},{6,5},{7,6},{8,7},{9,8},{10,9},{11,1... | collective-permute-start | bytes 6152 | tf_op jit(solution)/shard_map/ppermute | solution.py:20
  38.4 7.8 collective-permute-start.2
  40.3 7.5 collective-permute-start.3
  51.4 29.8 %collective-permute-start.4 = (bf16[4,1,256]{2,0,1:T(4,128)(2,1)S(1)}, bf16[4,1,256]{2,0,1:T(4,128)(2,1)S(1)}, u32[]{:S(2)}, u32[]{:S(2)}) collective-permute-start(bf16[4,1,256]{2,0,1:T(4,128)(2,1)S(1)} %get-tuple-element.114), channel_id=1, source_target_pairs={{0,1},{1,2},{2,3},{3,4},{4,5},{5,6},{6,7},{7,8},{8,9},{9,10},{10,1... | collective-permute-start | bytes 6152 | tf_op jit(solution)/shard_map/ppermute | solution.py:18
  73.1 9.4 collective-permute-start.5
  82.6 7.7 collective-permute-start.6
  84.6 7.5 collective-permute-start.7
  95.7 11.1 collective-permute-start.8
  98.4 9.7 collective-permute-start.9
  108.2 7.8 collective-permute-start.10
  110.1 7.5 collective-permute-start.11
  122.2 21.1 %all-to-all-start = ((bf16[32,2,720]{2,1,0:T(2,128)(2,1)}), bf16[32,2,720]{2,1,0:T(2,128)(2,1)S(1)}, u32[]{:S(2)}, u32[]{:S(2)}) async-start(bf16[32,2,720]{2,1,0:T(2,128)(2,1)} %reshape.155), calls=%async_computation | async-start | bytes 196608 | tf_op jit(solution)/shard_map/all_to_all | solution.py:89
  143.9 7.3 slice-start
  158.1 42.2 %copy-start.1 = (bf16[9,64,64]{1,2,0:T(8,128)(2,1)S(1)}, bf16[9,64,64]{1,2,0:T(8,128)(2,1)}, u32[]{:S(2)}) copy-start(bf16[9,64,64]{1,2,0:T(8,128)(2,1)} %get-tuple-element.32) | copy-start | bytes 221188
  160.0 16.3 all-to-all-start.1
  180.9 10.1 collective-permute-start.12
  183.7 8.6 collective-permute-start.13
  192.4 8.7 collective-permute-start.14
  194.3 7.5 collective-permute-start.15
  205.5 10.3 collective-permute-start.16
  207.4 9.7 collective-permute-start.17
  217.2 8.5 collective-permute-start.18
  219.1 7.5 collective-permute-start.19
  227.4 21.4 %copy-start = (f32[4,45,256]{2,0,1:T(4,128)S(1)}, f32[4,45,256]{2,0,1:T(4,128)}, u32[]{:S(2)}) copy-start(f32[4,45,256]{2,0,1:T(4,128)} %param.5) | copy-start | bytes 552964
  229.4 10.3 collective-permute-start.20
  231.3 9.7 collective-permute-start.21
  241.1 11.6 collective-permute-start.22
  243.1 9.7 collective-permute-start.23
  358.3 1490.8 %copy-start.5 = (f32[16,4]{0,1:T(4,128)}, f32[16,4]{0,1:T(4,128)S(1)}, u32[]{:S(2)}) copy-start(f32[16,4]{0,1:T(4,128)S(1)} %get-tuple-element.28) | copy-start | bytes 772
  (2 other events, 8.8 us)
